TPU v7x, 32 devices: a whole 2x2x4 slice. The times are simulated.
32 devices in a mesh: shot: 8 (over z, y), rcv: 4 (over x, core).
Axes of the slice: x: 2, y: 2, z: 4, core: 2. Of those that a mesh axis runs over, the one named last changes fastest.
Arguments:
- data_matrix: bfloat16 [2, 16, 1024, 1024], P(None, None, 'shot', 'rcv'), may hold values from -12 to 12
- shot_records: bfloat16 [2, 16, 1024, 1024], P(None, None, 'rcv', 'shot'), may hold values from -4 to 4
- live: int32 [1024, 1024], P('rcv', 'shot'), may hold values 0 or 1
Outputs:
- predicted: bfloat16 [2, 16, 1024, 1024], P(None, None, 'rcv', 'shot')
- primaries: bfloat16 [2, 16, 1024, 1024], P(None, None, 'rcv', 'shot')
All inputs are finite; a program needn't handle non-finite values. No bound on the sum of `live` on one device may be relied on, other than what follows from the above.
Results may differ from a plain program's by a relative error of at most 0.013.
Values may be sent and summed in bfloat16 or wider, within the bound.
A program may use at most 128 MiB of HBM per device.

v0:
```python
import jax
import jax.numpy as jnp
from jax import lax
from jax.sharding import PartitionSpec as P


def complex_product(left, right):
    prod = jnp.einsum("afrk,bfks->abfrs", left, right, preferred_element_type=jnp.float32)
    return jnp.stack((prod[0, 0] - prod[1, 1], prod[0, 1] + prod[1, 0]))


def shards(data_matrix, shot_records, live):
    records = shot_records * live.astype(jnp.bfloat16)[None, None]
    own_rows = records.shape[2]
    partial_terms = complex_product(
        lax.all_gather(data_matrix, "shot", axis=2, tiled=True), records
    )
    summed = lax.psum(partial_terms.astype(jnp.bfloat16), "rcv").astype(jnp.float32)
    total = lax.dynamic_slice_in_dim(summed, lax.axis_index("rcv") * own_rows, own_rows, 2)
    rec = records.astype(jnp.float32)
    num_re = jnp.sum(total[0] * rec[0] + total[1] * rec[1], axis=1)
    num_im = jnp.sum(total[0] * rec[1] - total[1] * rec[0], axis=1)
    power = jnp.sum(total[0] * total[0] + total[1] * total[1], axis=1)
    sum_re, sum_im, sum_power = lax.psum((num_re, num_im, power), "rcv")
    points = float(own_rows * lax.axis_size("rcv"))
    power_mean = sum_power / points + 1e-06
    filt_re = (sum_re / points / power_mean)[:, None, :]
    filt_im = (sum_im / points / power_mean)[:, None, :]
    out_re = rec[0] - (filt_re * total[0] - filt_im * total[1])
    out_im = rec[1] - (filt_re * total[1] + filt_im * total[0])
    primaries = jnp.stack((out_re, out_im)).astype(jnp.bfloat16)
    return (total.astype(jnp.bfloat16), primaries)


def solution(mesh):
    in_specs = (P(None, None, "shot", "rcv"), P(None, None, "rcv", "shot"), P("rcv", "shot"))
    out_specs = (P(None, None, "rcv", "shot"), P(None, None, "rcv", "shot"))
    return jax.shard_map(shards, mesh=mesh, in_specs=in_specs, out_specs=out_specs, check_vma=False)
```

profile of v0, /device:TPU:15, one launch (start us, length us, event | category | flops | bytes accessed | tf_op | source)
XLA Modules:
  0.0 463.8 jit_solution(6643771911731964899)
XLA Ops:
  7.2 0.0 all-gather.2.cloned.1.call-start
  7.2 3.1 copy.7
  10.3 0.0 copy-start
  10.3 0.0 all-gather.2.cloned.1.call-update
  10.4 0.0 copy-start.1
  10.4 0.0 all-reduce.3.cloned.1.call-start
  10.4 1.5 copy-done
  11.9 2.6 copy.6
  14.5 0.0 copy-done.1
  14.5 0.1 copy.5
  14.6 4.0 multiply_convert_fusion
  18.7 217.6 %all-gather.2.cloned.1.call-done = bf16[2,16,1024,256]{3,2,0,1:T(8,128)(2,1)} async-done(((bf16[2,16,128,256]{3,2,0,1:T(8,128)(2,1)}), bf16[2,16,1024,256]{3,2,0,1:T(8,128)(2,1)}) %all-gather.2.cloned.1.call-update) | async-done | bytes 16777232 | tf_op jit(solution)/shard_map/all_gather | solution.py:16
  236.3 17.6 %fusion.2 = f32[2,2,16,1024,128]{3,4,0,1,2:T(8,128)} fusion(bf16[2,16,1024,256]{3,2,0,1:T(8,128)(2,1)} %all-gather.2.cloned.1.call-done, bf16[2,16,256,128,1]{2,3,1,0,4:T(8,128)(2,1)S(1)} %get-tuple-element.15), kind=kOutput, calls=%fused_computation.2 | convolution fusion | flops 4294967296 | bytes 52428800 | tf_op jit(solution)/shard_map/afrk,bfks->abfrs/dot_general | solution.py:8
  253.9 6.6 %fusion.9 = bf16[1,16,1024,128]{2,3,1,0:T(8,128)(2,1)S(1)} fusion(f32[2,2,16,1024,128]{3,4,0,1,2:T(8,128)} %fusion.2), kind=kLoop, calls=%fused_computation.11 | loop fusion | flops 4194304 | bytes 20971520 | tf_op jit(solution)/shard_map/add | solution.py:9
  260.5 8.8 %fusion.8 = bf16[1,16,1024,128]{2,3,1,0:T(8,128)(2,1)} fusion(f32[2,2,16,1024,128]{3,4,0,1,2:T(8,128)} %fusion.2), kind=kLoop, calls=%fused_computation.10 | loop fusion | flops 4194304 | bytes 20971520 | tf_op jit(solution)/shard_map/sub | solution.py:9
  269.3 6.2 %pad_maximum_fusion = bf16[2,16,1024,128]{2,3,1,0:T(8,128)(2,1)} fusion(bf16[1,16,1024,128]{2,3,1,0:T(8,128)(2,1)S(1)} %fusion.9, bf16[1,16,1024,128]{2,3,1,0:T(8,128)(2,1)} %fusion.8), kind=kLoop, calls=%fused_computation.9 | loop fusion | flops 4194304 | bytes 16777216 | tf_op jit(solution)/shard_map/stack | solution.py:9
  275.4 0.0 all-reduce.3.cloned.1.call-update
  275.5 153.7 %all-reduce.3.cloned.1.call-done = bf16[2,16,1024,128]{2,3,1,0:T(8,128)(2,1)} async-done(((bf16[2,16,1024,128]{2,3,1,0:T(8,128)(2,1)}), bf16[2,16,1024,128]{2,3,1,0:T(8,128)(2,1)}) %all-reduce.3.cloned.1.call-update) | async-done | bytes 8388624 | tf_op jit(solution)/shard_map/psum | solution.py:18
  429.2 4.1 dynamic-slice_convert_fusion
  433.3 2.4 copy.11
  435.7 4.6 add_reduce_fusion.1
  440.3 10.2 %all-reduce = (f32[16,128]{1,0:T(8,128)S(1)}, f32[16,128]{1,0:T(8,128)S(1)}, f32[16,128]{1,0:T(8,128)S(1)}) all-reduce(f32[16,128]{1,0:T(8,128)S(1)} %get-tuple-element.5, f32[16,128]{1,0:T(8,128)S(1)} %get-tuple-element.6, f32[16,128]{1,0:T(8,128)S(1)} %get-tuple-element.4), channel_id=1, replica_groups=mesh['shot'=8,'rcv'=4] {'rcv'}, use_global_device_ids=true, to_apply=%region_6.0 | all-reduce | flops 6144 | bytes 49152 | tf_op jit(solution)/shard_map/psum | solution.py:24
  450.6 3.8 subtract_convert_fusion.1
  454.4 0.2 pad_maximum_fusion.1
  454.6 2.4 copy.12
  (2 shorter events, 0.0 us)
Async XLA Ops:
  7.2 229.1 %all-gather.2.cloned.1.call-start = ((), (), s32[]{:S(2)}) async-start(), calls=%async_computation | async-start | bytes 18874368 | tf_op jit(solution)/shard_map/all_gather | solution.py:16
  10.3 1.6 copy-start
  10.4 4.1 copy-start.1
  10.4 418.8 %all-reduce.3.cloned.1.call-start = ((), (), s32[]{:S(2)}) async-start(), calls=%async_computation.1 | async-start | bytes 16777216 | tf_op jit(solution)/shard_map/psum | solution.py:18
Sparse Core Ops, SparseCore 0:
  10.8 225.5 all-gather.1
  275.6 153.5 all-reduce.2
where the time goes:
time: 466 us; the launch traced here: 464 us
  waiting for transfers between devices  371 us (80%)
  other arithmetic  38.4 us (8%)
  matrix products  17.6 us (4%)
  between operations  14.1 us (3%)
  local copies, waits for them, and re-layouts  12.1 us (3%)
  blocking collectives  10.2 us (2%)
    all_gather x1, waiting for transfers between devices, shards(): lax.all_gather(data_matrix, 'shot', axis=2, tiled=True)  218 us
    psum x1, waiting for transfers between devices, shards(): lax.psum(partial_terms.astype(jnp.bfloat16), 'rcv').astype(jnp.float32)  154 us
    dot_general x1, matrix products, complex_product(): jnp.einsum('afrk,bfks->abfrs', left, right, preferred_element_type=jnp.fl...  17.6 us
    unnamed x8, local copies, waits for them, and re-layouts  12 us
    psum x1, blocking collectives, shards(): sum_re, sum_im, sum_power = lax.psum((num_re, num_im, power), 'rcv')  10.2 us
  transfers between devices with their start and end apart: 2, of which 2 were waited for; matrix products, arithmetic and copies ran while one was open for 1% of the time, Pallas kernels for 0%

commit v1 on v0

v1 whole, which is shorter than its diff:
```python
import functools

import jax
import jax.numpy as jnp
from jax import lax
from jax.experimental import pallas as pl
from jax.experimental.pallas import tpu as pltpu
from jax.sharding import PartitionSpec as P

MESH = pl.DeviceIdType.MESH


def each(start, stop, body):
    def step(index, carry):
        body(index)
        return carry

    lax.fori_loop(start, stop, step, 0)


def exchange_kernel(
    n_shot, n_rcv,
    d_ref, s_ref, live_ref, o_ref, filt_ref,
    dbuf, pbuf, srec, live_v, rec, mbuf, fbuf,
    load_sem, d_send, d_recv, p_send, p_recv, o_send, o_recv, f_send, f_recv,
):
    n_freq, own_rows = d_ref.shape[1], d_ref.shape[2]
    own_pts, own_shots = s_ref.shape[2], s_ref.shape[3]
    points = own_pts * n_rcv
    per_group = n_freq // n_rcv
    n_groups = n_shot // per_group
    me_i, me_j = lax.axis_index("shot"), lax.axis_index("rcv")
    group, place = lax.div(me_i, per_group), lax.rem(me_i, per_group)
    my_f = place * n_rcv + me_j
    me = me_i * n_rcv + me_j
    n_dev = n_shot * n_rcv

    load_s = pltpu.make_async_copy(s_ref, srec, load_sem.at[0])
    load_live = pltpu.make_async_copy(live_ref, live_v, load_sem.at[1])
    load_s.start()
    load_live.start()

    barrier = pltpu.get_barrier_semaphore()

    def greet(k):
        other = lax.rem(me + k, n_dev)
        pl.semaphore_signal(
            barrier, inc=1, device_id=(lax.div(other, n_rcv), lax.rem(other, n_rcv)), device_id_type=MESH
        )

    each(1, n_dev, greet)
    pl.semaphore_wait(barrier, n_dev - 1)

    def home(g, f):
        return (g * per_group + lax.div(f, n_rcv), lax.rem(f, n_rcv))

    def d_dst(i, j):
        return dbuf.at[j, :, pl.ds(pl.multiple_of(i * own_rows, own_rows), own_rows), :]

    def d_copy(m):
        f = lax.rem(my_f + lax.div(m, n_groups), n_freq)
        g = lax.rem(group + lax.rem(m, n_groups), n_groups)
        return pltpu.make_async_remote_copy(
            src_ref=d_ref.at[:, f], dst_ref=d_dst(me_i, me_j), send_sem=d_send.at[m], recv_sem=d_recv.at[me],
            device_id=home(g, f), device_id_type=MESH,
        )

    def p_dst(b, j):
        return pbuf.at[b, pl.ds(pl.multiple_of(j * own_pts, own_pts), own_pts), :]

    def p_copy(k):
        f = lax.rem(my_f + k, n_freq)
        return pltpu.make_async_remote_copy(
            src_ref=rec.at[f], dst_ref=p_dst(place, me_j), send_sem=p_send.at[k], recv_sem=p_recv.at[my_f],
            device_id=home(group, f), device_id_type=MESH,
        )

    pltpu.make_async_copy(d_ref.at[:, my_f], d_dst(me_i, me_j), d_recv.at[me]).start()
    each(1, n_groups * n_freq, lambda m: d_copy(m).start())

    load_s.wait()
    load_live.wait()

    def mask(f):
        keep = live_v[...].astype(jnp.bfloat16)
        rec[f, :, :own_shots] = srec[0, f] * keep
        rec[f, :, own_shots:] = srec[1, f] * keep

    mask(my_f)
    pltpu.make_async_copy(rec.at[my_f], p_dst(place, me_j), p_recv.at[my_f]).start()

    def send_p(k):
        mask(lax.rem(my_f + k, n_freq))
        p_copy(k).start()

    each(1, n_freq, send_p)

    def p_arrived(n):
        dst = p_dst(lax.div(n, n_rcv), lax.rem(n, n_rcv))
        pltpu.make_async_copy(dst, dst, p_recv.at[n]).wait()

    def d_arrived(n):
        dst = d_dst(lax.div(n, n_rcv), lax.rem(n, n_rcv))
        pltpu.make_async_copy(dst, dst, d_recv.at[n]).wait()

    each(0, n_freq, p_arrived)
    each(0, n_dev, d_arrived)

    def turn(kb, jj):
        return lax.rem(place + kb, per_group), lax.rem(me_j + jj, n_rcv)

    def o_src(b, j):
        return mbuf.at[b, pl.ds(pl.multiple_of(j * own_pts, own_pts), own_pts), :]

    def o_copy(n):
        b, j = turn(lax.div(n, n_rcv), lax.rem(n, n_rcv))
        return pltpu.make_async_remote_copy(
            src_ref=o_src(b, j), dst_ref=o_ref.at[my_f], send_sem=o_send.at[n], recv_sem=o_recv.at[my_f],
            device_id=(group * per_group + b, j), device_id_type=MESH,
        )

    def f_copy(n):
        b, j = turn(lax.div(n, n_rcv), lax.rem(n, n_rcv))
        return pltpu.make_async_remote_copy(
            src_ref=fbuf.at[b], dst_ref=filt_ref.at[my_f], send_sem=f_send.at[n], recv_sem=f_recv.at[my_f],
            device_id=(group * per_group + b, j), device_id_type=MESH,
        )

    def shot_block(kb):
        def row_tile(jj, sums):
            b, j = turn(kb, jj)
            rows = pl.ds(pl.multiple_of(j * own_pts, own_pts), own_pts)
            left = right = None
            for h in range(n_rcv):
                block = pbuf[b, h * own_pts:(h + 1) * own_pts, :]
                one = jnp.dot(dbuf[h, 0, rows, :], block, preferred_element_type=jnp.float32)
                two = jnp.dot(dbuf[h, 1, rows, :], block, preferred_element_type=jnp.float32)
                left = one if left is None else left + one
                right = two if right is None else right + two
            m_re = left[:, :own_shots] - right[:, own_shots:]
            m_im = left[:, own_shots:] + right[:, :own_shots]
            mbuf[b, rows, :own_shots] = m_re.astype(jnp.bfloat16)
            mbuf[b, rows, own_shots:] = m_im.astype(jnp.bfloat16)
            n = kb * n_rcv + jj

            @pl.when(n == 0)
            def _():
                pltpu.make_async_copy(o_src(b, j), o_ref.at[my_f], o_recv.at[my_f]).start()

            @pl.when(n > 0)
            def _():
                o_copy(n).start()

            p_re = pbuf[b, rows, :own_shots].astype(jnp.float32)
            p_im = pbuf[b, rows, own_shots:].astype(jnp.float32)

            def down(value):
                return jnp.sum(value.reshape(own_pts // 8, 8, own_shots), axis=0)

            return (
                sums[0] + down(m_re * p_re + m_im * p_im),
                sums[1] + down(m_re * p_im - m_im * p_re),
                sums[2] + down(m_re * m_re + m_im * m_im),
            )

        zero = jnp.zeros((8, own_shots), jnp.float32)
        sums = lax.fori_loop(0, n_rcv, row_tile, (zero, zero, zero))
        num_re, num_im, power = (jnp.sum(v, axis=0, keepdims=True) / float(points) for v in sums)
        power = power + 1e-6
        row = lax.broadcasted_iota(jnp.int32, (8, own_shots), 0)
        b, _ = turn(kb, 0)
        fbuf[b] = jnp.where(row < 4, num_re / power, num_im / power)

        @pl.when(kb == 0)
        def _():
            pltpu.make_async_copy(fbuf.at[b], filt_ref.at[my_f], f_recv.at[my_f]).start()

        @pl.when(kb > 0)
        def _():
            f_copy(kb * n_rcv).start()

        each(1, n_rcv, lambda jj: f_copy(kb * n_rcv + jj).start())

    each(0, per_group, shot_block)

    def result_arrived(n):
        pltpu.make_async_copy(o_ref.at[n], o_ref.at[n], o_recv.at[n]).wait()
        pltpu.make_async_copy(filt_ref.at[n], filt_ref.at[n], f_recv.at[n]).wait()

    each(0, n_freq, result_arrived)

    each(1, n_groups * n_freq, lambda m: d_copy(m).wait_send())
    each(1, n_freq, lambda k: p_copy(k).wait_send())
    each(1, n_freq, lambda n: o_copy(n).wait_send())
    each(1, n_freq, lambda n: f_copy(n).wait_send())


def subtract_kernel(o_ref, filt_ref, s_ref, live_ref, pred_ref, prim_ref):
    shots = s_ref.shape[3]
    keep = live_ref[...].astype(jnp.bfloat16)
    for f in range(o_ref.shape[0]):
        re, im = o_ref[f, :, :shots], o_ref[f, :, shots:]
        pred_ref[0, f] = re
        pred_ref[1, f] = im
        re, im = re.astype(jnp.float32), im.astype(jnp.float32)
        filt_re, filt_im = filt_ref[f, 0:1, :], filt_ref[f, 4:5, :]
        rec_re = (s_ref[0, f] * keep).astype(jnp.float32)
        rec_im = (s_ref[1, f] * keep).astype(jnp.float32)
        prim_ref[0, f] = (rec_re - (filt_re * re - filt_im * im)).astype(jnp.bfloat16)
        prim_ref[1, f] = (rec_im - (filt_re * im + filt_im * re)).astype(jnp.bfloat16)


def shards(n_shot, n_rcv, data_matrix, shot_records, live):
    _, n_freq, own_rows, own_pts = data_matrix.shape
    own_shots = shot_records.shape[3]
    points = own_pts * n_rcv
    per_group = n_freq // n_rcv
    n_groups = n_shot // per_group
    anywhere = pl.BlockSpec(memory_space=pl.ANY)
    dma = pltpu.SemaphoreType.DMA
    multiples, filt = pl.pallas_call(
        functools.partial(exchange_kernel, n_shot, n_rcv),
        out_shape=(
            jax.ShapeDtypeStruct((n_freq, own_pts, 2 * own_shots), jnp.bfloat16),
            jax.ShapeDtypeStruct((n_freq, 8, own_shots), jnp.float32),
        ),
        in_specs=[anywhere] * 3,
        out_specs=(anywhere, anywhere),
        scratch_shapes=[
            pltpu.VMEM((n_rcv, 2, points, own_pts), jnp.bfloat16),
            pltpu.VMEM((per_group, points, 2 * own_shots), jnp.bfloat16),
            pltpu.VMEM((2, n_freq, own_pts, own_shots), jnp.bfloat16),
            pltpu.VMEM((own_pts, own_shots), jnp.int32),
            pltpu.VMEM((n_freq, own_pts, 2 * own_shots), jnp.bfloat16),
            pltpu.VMEM((per_group, points, 2 * own_shots), jnp.bfloat16),
            pltpu.VMEM((per_group, 8, own_shots), jnp.float32),
            dma((2,)),
            dma((n_groups * n_freq,)),
            dma((n_shot * n_rcv,)),
            dma((n_freq,)),
            dma((n_freq,)),
            dma((n_freq,)),
            dma((n_freq,)),
            dma((n_freq,)),
            dma((n_freq,)),
        ],
        compiler_params=pltpu.CompilerParams(
            collective_id=0, has_side_effects=True, vmem_limit_bytes=32 * 1024 * 1024
        ),
    )(data_matrix, shot_records, live)
    step = 4
    pair = pl.BlockSpec((2, step, own_pts, own_shots), lambda f: (0, f, 0, 0))
    out = jax.ShapeDtypeStruct((2, n_freq, own_pts, own_shots), jnp.bfloat16)
    return pl.pallas_call(
        subtract_kernel,
        grid=(n_freq // step,),
        out_shape=(out, out),
        in_specs=[
            pl.BlockSpec((step, own_pts, 2 * own_shots), lambda f: (f, 0, 0)),
            pl.BlockSpec((step, 8, own_shots), lambda f: (f, 0, 0)),
            pair,
            pl.BlockSpec((own_pts, own_shots), lambda f: (0, 0)),
        ],
        out_specs=(pair, pair),
        compiler_params=pltpu.CompilerParams(vmem_limit_bytes=24 * 1024 * 1024),
    )(multiples, filt, shot_records, live)


def solution(mesh):
    in_specs = (P(None, None, "shot", "rcv"), P(None, None, "rcv", "shot"), P("rcv", "shot"))
    out_specs = (P(None, None, "rcv", "shot"), P(None, None, "rcv", "shot"))
    body = functools.partial(shards, mesh.shape["shot"], mesh.shape["rcv"])
    return jax.shard_map(body, mesh=mesh, in_specs=in_specs, out_specs=out_specs, check_vma=False)
```

time: 466 us -> 156 us (0.33)
  the two profiles are of different devices: /device:TPU:15 before, /device:TPU:5 now
where the time goes in v1:
time: 156 us; the launch traced here: 155 us
  Pallas kernels  151 us (97%)
  local copies, waits for them, and re-layouts  4.08 us (3%)
    pallas_call x1, Pallas kernels, shards(): pl.pallas_call(functools.partial(exchange_kernel, n_shot, n_rcv), out_sha...  148 us
    unnamed x6, local copies, waits for them, and re-layouts  4.08 us
    pallas_call x1, Pallas kernels, shards(): pl.pallas_call(subtract_kernel, grid=(n_freq // step,), out_shape=(out, o...  3.2 us

profile of v1, /device:TPU:5, one launch (start us, length us, event | category | flops | bytes accessed | tf_op | source)
XLA Modules:
  0.0 155.4 jit_solution(8252620711251471288)
XLA Ops:
  0.6 0.0 copy-start
  0.6 1.6 %copy-done = bf16[2,16,256,128]{3,2,1,0:T(8,128)(2,1)S(1)} copy-done((bf16[2,16,256,128]{3,2,1,0:T(8,128)(2,1)S(1)}, bf16[2,16,256,128]{3,2,1,0:T(8,128)(2,1)}, u32[]{:S(2)}) %copy-start) | copy-done | bytes 2097176
  2.2 0.0 copy-start.1
  2.2 1.6 %copy-done.1 = bf16[2,16,128,256]{3,2,1,0:T(8,128)(2,1)S(1)} copy-done((bf16[2,16,128,256]{3,2,1,0:T(8,128)(2,1)S(1)}, bf16[2,16,128,256]{3,2,1,0:T(8,128)(2,1)}, u32[]{:S(2)}) %copy-start.1) | copy-done | bytes 2097176
  3.8 0.0 copy-start.2
  3.8 0.9 copy-done.2
  4.7 147.5 %shard_map.50 = (bf16[16,256,256]{2,1,0:T(8,128)(2,1)S(1)}, f32[16,8,128]{2,1,0:T(8,128)S(1)}) custom-call(bf16[2,16,128,256]{3,2,1,0:T(8,128)(2,1)S(1)} %copy-done.1, bf16[2,16,256,128]{3,2,1,0:T(8,128)(2,1)S(1)} %copy-done, s32[256,128]{1,0:T(8,128)S(1)} %copy-done.2), custom_call_target="tpu_custom_call" | custom-call | tf_op jit(solution)/shard_map/pallas_call | solution.py:221
  152.2 3.2 %shard_map.51 = (bf16[2,16,256,128]{3,2,1,0:T(8,128)(2,1)}, bf16[2,16,256,128]{3,2,1,0:T(8,128)(2,1)}) custom-call(bf16[16,256,256]{2,1,0:T(8,128)(2,1)S(1)} %get-tuple-element.4.o_ref, f32[16,8,128]{2,1,0:T(8,128)S(1)} %get-tuple-element.5.filt_ref, bf16[2,16,256,128]{3,2,1,0:T(8,128)(2,1)S(1)} %copy-done, s32[256,128]{1,0:T(8,128)S(1)} %copy-done.2), custom_call_target="tpu_custom_call" | custom-call | tf_op jit(solution)/shard_map/pallas_call | solution.py:254
Async XLA Ops:
  0.6 1.6 %copy-start = (bf16[2,16,256,128]{3,2,1,0:T(8,128)(2,1)S(1)}, bf16[2,16,256,128]{3,2,1,0:T(8,128)(2,1)}, u32[]{:S(2)}) copy-start(bf16[2,16,256,128]{3,2,1,0:T(8,128)(2,1)} %s_ref.3) | copy-start | bytes 6291460
  2.2 1.6 %copy-start.1 = (bf16[2,16,128,256]{3,2,1,0:T(8,128)(2,1)S(1)}, bf16[2,16,128,256]{3,2,1,0:T(8,128)(2,1)}, u32[]{:S(2)}) copy-start(bf16[2,16,128,256]{3,2,1,0:T(8,128)(2,1)} %d_ref.1) | copy-start | bytes 6291460
  3.8 0.9 copy-start.2

commit v2 on v1

v2 whole, which is shorter than its diff:
```python
import functools

import jax
import jax.numpy as jnp
from jax import lax
from jax.experimental import pallas as pl
from jax.experimental.pallas import tpu as pltpu
from jax.sharding import PartitionSpec as P

MESH = pl.DeviceIdType.MESH


def each(start, stop, body):
    def step(index, carry):
        body(index)
        return carry

    lax.fori_loop(start, stop, step, 0)


def exchange_kernel(
    n_shot, n_rcv,
    d_ref, s_ref, live_ref, o_ref, filt_ref,
    dbuf, pbuf, srec, live_v, rec, mbuf, fbuf, acc,
    load_sem, d_send, d_recv, r_send, p_send, p_recv, o_send, o_recv, f_send, f_recv,
):
    n_freq, own_rows = d_ref.shape[1], d_ref.shape[2]
    own_pts, own_shots = s_ref.shape[2], s_ref.shape[3]
    points = own_pts * n_rcv
    per_group = n_freq // n_rcv
    half = per_group // 2
    n_each = n_freq // (half * n_rcv)
    n_groups = n_shot // per_group
    n_dev = n_shot * n_rcv
    me_i, me_j = lax.axis_index("shot"), lax.axis_index("rcv")
    group, place = lax.div(me_i, per_group), lax.rem(me_i, per_group)
    me = me_i * n_rcv + me_j
    column = lax.rem(place, half)

    def base(g):
        return half * (1 - lax.rem(g, 2))

    computes = lax.div(place, half) == lax.div(base(group), half)

    load_s = pltpu.make_async_copy(s_ref, srec, load_sem.at[0])
    load_live = pltpu.make_async_copy(live_ref, live_v, load_sem.at[1])
    load_s.start()
    load_live.start()

    barrier = pltpu.get_barrier_semaphore()

    def greet(k):
        other = lax.rem(me + k, n_dev)
        pl.semaphore_signal(
            barrier, inc=1, device_id=(lax.div(other, n_rcv), lax.rem(other, n_rcv)), device_id_type=MESH
        )

    each(1, n_dev, greet)
    pl.semaphore_wait(barrier, n_dev - 1)

    def rows_of(i, size):
        return pl.ds(pl.multiple_of(i * size, size), size)

    def send(src, dst, target, send_sem, recv_sem):
        here = jnp.logical_and(target[0] == me_i, target[1] == me_j)

        @pl.when(here)
        def _():
            pltpu.make_async_copy(src, dst, recv_sem).start()

        @pl.when(jnp.logical_not(here))
        def _():
            pltpu.make_async_remote_copy(
                src_ref=src, dst_ref=dst, send_sem=send_sem, recv_sem=recv_sem,
                device_id=target, device_id_type=MESH,
            ).start()

    def sent(src, target, send_sem):
        here = jnp.logical_and(target[0] == me_i, target[1] == me_j)

        @pl.when(jnp.logical_not(here))
        def _():
            pltpu.make_async_copy(src, src, send_sem).wait()

    def arrived(dst, recv_sem):
        pltpu.make_async_copy(dst, dst, recv_sem).wait()

    def target_of(m):
        c = lax.rem(column + lax.div(m, n_rcv * n_each), half)
        j = lax.rem(me_j + lax.rem(lax.div(m, n_each), n_rcv), n_rcv)
        fi = lax.rem(m, n_each)
        return (group * per_group + base(group) + c, j), fi, (c * n_rcv + j) * n_each + fi

    def d_block(fi, i, j):
        return dbuf.at[fi, j, :, rows_of(i, own_rows), :]

    def send_d(m):
        target, fi, f = target_of(m)
        send(d_ref.at[:, f], d_block(fi, me_i, me_j), target, d_send.at[m], d_recv.at[fi, me_i, me_j])

    def sent_d(m):
        target, _, f = target_of(m)
        sent(d_ref.at[:, f], target, d_send.at[m])

    def send_p(m):
        target, fi, f = target_of(m)
        keep = live_v[...].astype(jnp.bfloat16)
        rec[f, :, :own_shots] = srec[0, f] * keep
        rec[f, :, own_shots:] = srec[1, f] * keep
        dst = pbuf.at[fi, place, rows_of(me_j, own_pts), :]
        send(rec.at[f], dst, target, p_send.at[m], p_recv.at[fi, place, me_j])

    def sent_p(m):
        target, _, f = target_of(m)
        sent(rec.at[f], target, p_send.at[m])

    @pl.when(computes)
    def _():
        each(0, n_freq, send_d)

    load_s.wait()
    load_live.wait()
    each(0, n_freq, send_p)

    first = n_freq - n_freq // 4

    @pl.when(jnp.logical_not(computes))
    def _():
        each(0, first, sent_p)
        each(0, n_freq, send_d)

    def partner(gg):
        g = lax.rem(group + gg, n_groups)
        return g, g * per_group + base(g) + column

    def position(g, t, far):
        near = base(g)
        return g * per_group + (half - near if far else near) + lax.rem(column + t, half)

    def relay_copy(fi, i, j, gg):
        _, target = partner(gg)
        return pltpu.make_async_remote_copy(
            src_ref=d_block(fi, i, j), dst_ref=d_block(fi, i, j),
            send_sem=r_send.at[gg - 1, fi, lax.rem(i, per_group), j], recv_sem=d_recv.at[fi, i, j],
            device_id=(target, me_j), device_id_type=MESH,
        )

    def relay(t, far, start, stop):
        i = position(group, t, far)

        def block(n):
            j = lax.rem(me_j + n_rcv - lax.div(n, n_each), n_rcv)
            fi = lax.rem(n, n_each)
            arrived(d_block(fi, i, j), d_recv.at[fi, i, j])
            each(1, n_groups, lambda gg: relay_copy(fi, i, j, gg).start())

        each(start * n_each, stop * n_each, block)

    def o_src(fi, b, i):
        return mbuf.at[fi, b, rows_of(i, own_rows), :]

    per_rcv = own_pts // own_rows

    def compute(i):
        rows = rows_of(i, own_rows)
        j = lax.div(i, per_rcv)

        def one(n):
            fi, b = lax.div(n, per_group), lax.rem(lax.rem(n, per_group) + place, per_group)
            total = None
            for h in range(n_rcv):
                block = pbuf[fi, b, h * own_pts:(h + 1) * own_pts, :]
                left = dbuf[fi, h, :, rows, :].reshape(2 * own_rows, own_pts)
                prod = jnp.dot(left, block, preferred_element_type=jnp.float32)
                total = prod if total is None else total + prod
            m_re = total[:own_rows, :own_shots] - total[own_rows:, own_shots:]
            m_im = total[:own_rows, own_shots:] + total[own_rows:, :own_shots]
            mbuf[fi, b, rows, :own_shots] = m_re.astype(jnp.bfloat16)
            mbuf[fi, b, rows, own_shots:] = m_im.astype(jnp.bfloat16)
            f = (column * n_rcv + me_j) * n_each + fi
            dst = o_ref.at[f, rows_of(lax.rem(i, per_rcv), own_rows), :]
            send(o_src(fi, b, i), dst, (group * per_group + b, j), o_send.at[fi, b, j], o_recv.at[f])
            p_re = pbuf[fi, b, rows, :own_shots].astype(jnp.float32)
            p_im = pbuf[fi, b, rows, own_shots:].astype(jnp.float32)

            def down(value):
                return jnp.sum(value.reshape(own_rows // 8, 8, own_shots), axis=0)

            acc[fi, b, 0] += down(m_re * p_re + m_im * p_im)
            acc[fi, b, 1] += down(m_re * p_im - m_im * p_re)
            acc[fi, b, 2] += down(m_re * m_re + m_im * m_im)

        each(0, n_each * per_group, one)

    def compute_others(t, far):
        def other(gg):
            g, _ = partner(gg)
            i = position(g, t, far)

            def block(n):
                j = lax.rem(me_j + n_rcv - lax.div(n, n_each), n_rcv)
                fi = lax.rem(n, n_each)
                arrived(d_block(fi, i, j), d_recv.at[fi, i, j])

            each(0, n_rcv * n_each, block)
            compute(i)

        each(1, n_groups, other)

    @pl.when(computes)
    def _():
        acc[...] = jnp.zeros_like(acc)
        for t in range(half):
            relay(t, False, 0, n_rcv)

        def records_arrived(n):
            fi, b, j = lax.div(n, per_group * n_rcv), lax.rem(lax.div(n, n_rcv), per_group), lax.rem(n, n_rcv)
            arrived(pbuf.at[fi, b, rows_of(j, own_pts), :], p_recv.at[fi, b, j])

        each(0, n_each * per_group * n_rcv, records_arrived)
        for t in range(half):
            compute(position(group, t, False))
        for t in range(half):
            compute_others(t, False)
        for t in range(half):
            relay(t, True, 0, n_rcv // 2)
            if t:
                compute_others(t - 1, True)
            relay(t, True, n_rcv // 2, n_rcv)
            compute(position(group, t, True))
        compute_others(half - 1, True)

        def f_args(n):
            fi, b, j = lax.div(n, per_group * n_rcv), lax.rem(lax.div(n, n_rcv), per_group), lax.rem(n, n_rcv)
            b = lax.rem(b + place, per_group)
            f = (column * n_rcv + me_j) * n_each + fi
            return fi, b, j, f, (group * per_group + b, j)

        def coefficients(n):
            fi, b = lax.div(n, per_group), lax.rem(n, per_group)
            num_re, num_im, power = (
                jnp.sum(acc[fi, b, v], axis=0, keepdims=True) / float(points) for v in range(3)
            )
            power = power + 1e-6
            row = lax.broadcasted_iota(jnp.int32, (8, own_shots), 0)
            fbuf[fi, b] = jnp.where(row < 4, num_re / power, num_im / power)

        each(0, n_each * per_group, coefficients)

        def send_f(n):
            fi, b, j, f, target = f_args(n)
            send(fbuf.at[fi, b], filt_ref.at[f], target, f_send.at[fi, b, j], f_recv.at[f])

        each(0, n_each * per_group * n_rcv, send_f)

        def sent_results(n):
            fi, b, j, _, target = f_args(n)
            sent(fbuf.at[fi, b], target, f_send.at[fi, b, j])
            sent(mbuf.at[fi, b, rows_of(j, own_pts), :], target, o_send.at[fi, b, j])

        each(0, n_each * per_group * n_rcv, sent_results)

        def sent_relays(n):
            gg = lax.div(n, n_each * per_group * n_rcv) + 1
            fi = lax.rem(lax.div(n, per_group * n_rcv), n_each)
            b, j = lax.rem(lax.div(n, n_rcv), per_group), lax.rem(n, n_rcv)
            relay_copy(fi, group * per_group + b, j, gg).wait_send()

        each(0, (n_groups - 1) * n_each * per_group * n_rcv, sent_relays)
        each(0, first, sent_p)

    def result_arrived(n):
        arrived(o_ref.at[n], o_recv.at[n])
        arrived(filt_ref.at[n], f_recv.at[n])

    each(0, n_freq, result_arrived)
    each(0, n_freq, sent_d)
    each(first, n_freq, sent_p)


def subtract_kernel(o_ref, filt_ref, s_ref, live_ref, pred_ref, prim_ref):
    shots = s_ref.shape[3]
    keep = live_ref[...].astype(jnp.bfloat16)
    for f in range(o_ref.shape[0]):
        re, im = o_ref[f, :, :shots], o_ref[f, :, shots:]
        pred_ref[0, f] = re
        pred_ref[1, f] = im
        re, im = re.astype(jnp.float32), im.astype(jnp.float32)
        filt_re, filt_im = filt_ref[f, 0:1, :], filt_ref[f, 4:5, :]
        rec_re = (s_ref[0, f] * keep).astype(jnp.float32)
        rec_im = (s_ref[1, f] * keep).astype(jnp.float32)
        prim_ref[0, f] = (rec_re - (filt_re * re - filt_im * im)).astype(jnp.bfloat16)
        prim_ref[1, f] = (rec_im - (filt_re * im + filt_im * re)).astype(jnp.bfloat16)


def shards(n_shot, n_rcv, data_matrix, shot_records, live):
    _, n_freq, own_rows, own_pts = data_matrix.shape
    own_shots = shot_records.shape[3]
    points = own_pts * n_rcv
    per_group = n_freq // n_rcv
    n_groups = n_shot // per_group
    n_each = n_freq // (per_group // 2 * n_rcv)
    anywhere = pl.BlockSpec(memory_space=pl.ANY)
    dma = pltpu.SemaphoreType.DMA
    multiples, filt = pl.pallas_call(
        functools.partial(exchange_kernel, n_shot, n_rcv),
        out_shape=(
            jax.ShapeDtypeStruct((n_freq, own_pts, 2 * own_shots), jnp.bfloat16),
            jax.ShapeDtypeStruct((n_freq, 8, own_shots), jnp.float32),
        ),
        in_specs=[anywhere] * 3,
        out_specs=(anywhere, anywhere),
        scratch_shapes=[
            pltpu.VMEM((n_each, n_rcv, 2, points, own_pts), jnp.bfloat16),
            pltpu.VMEM((n_each, per_group, points, 2 * own_shots), jnp.bfloat16),
            pltpu.VMEM((2, n_freq, own_pts, own_shots), jnp.bfloat16),
            pltpu.VMEM((own_pts, own_shots), jnp.int32),
            pltpu.VMEM((n_freq, own_pts, 2 * own_shots), jnp.bfloat16),
            pltpu.VMEM((n_each, per_group, points, 2 * own_shots), jnp.bfloat16),
            pltpu.VMEM((n_each, per_group, 8, own_shots), jnp.float32),
            pltpu.VMEM((n_each, per_group, 3, 8, own_shots), jnp.float32),
            dma((2,)),
            dma((n_freq,)),
            dma((n_each, n_shot, n_rcv)),
            dma((n_groups - 1, n_each, per_group, n_rcv)),
            dma((n_freq,)),
            dma((n_each, per_group, n_rcv)),
            dma((n_each, per_group, n_rcv)),
            dma((n_freq,)),
            dma((n_each, per_group, n_rcv)),
            dma((n_freq,)),
        ],
        compiler_params=pltpu.CompilerParams(
            collective_id=0, has_side_effects=True, vmem_limit_bytes=40 * 1024 * 1024
        ),
    )(data_matrix, shot_records, live)
    step = 4
    pair = pl.BlockSpec((2, step, own_pts, own_shots), lambda f: (0, f, 0, 0))
    out = jax.ShapeDtypeStruct((2, n_freq, own_pts, own_shots), jnp.bfloat16)
    return pl.pallas_call(
        subtract_kernel,
        grid=(n_freq // step,),
        out_shape=(out, out),
        in_specs=[
            pl.BlockSpec((step, own_pts, 2 * own_shots), lambda f: (f, 0, 0)),
            pl.BlockSpec((step, 8, own_shots), lambda f: (f, 0, 0)),
            pair,
            pl.BlockSpec((own_pts, own_shots), lambda f: (0, 0)),
        ],
        out_specs=(pair, pair),
        compiler_params=pltpu.CompilerParams(vmem_limit_bytes=24 * 1024 * 1024),
    )(multiples, filt, shot_records, live)


def solution(mesh):
    in_specs = (P(None, None, "shot", "rcv"), P(None, None, "rcv", "shot"), P("rcv", "shot"))
    out_specs = (P(None, None, "rcv", "shot"), P(None, None, "rcv", "shot"))
    body = functools.partial(shards, mesh.shape["shot"], mesh.shape["rcv"])
    return jax.shard_map(body, mesh=mesh, in_specs=in_specs, out_specs=out_specs, check_vma=False)
```

time: 156 us -> 186 us (1.19)
  the two profiles are of different devices: /device:TPU:5 before, /device:TPU:15 now
where the time goes in v2:
time: 186 us; the launch traced here: 182 us
  Pallas kernels  177 us (95%)
  local copies, waits for them, and re-layouts  4.08 us (2%)
    pallas_call x1, Pallas kernels, shards(): pl.pallas_call(functools.partial(exchange_kernel, n_shot, n_rcv), out_sha...  174 us
    unnamed x6, local copies, waits for them, and re-layouts  4.08 us

profile of v2, /device:TPU:15, one launch (start us, length us, event | category | flops | bytes accessed | tf_op | source)
XLA Modules:
  0.0 182.1 jit_solution(1654252414541104706)
XLA Ops:
  0.6 0.0 copy-start
  0.6 1.6 copy-done
  2.2 0.0 copy-start.1
  2.2 1.6 copy-done.1
  3.8 0.0 copy-start.2
  3.8 0.9 copy-done.2
  4.7 174.2 %shard_map.50 = (bf16[16,256,256]{2,1,0:T(8,128)(2,1)S(1)}, f32[16,8,128]{2,1,0:T(8,128)S(1)}) custom-call(bf16[2,16,128,256]{3,2,1,0:T(8,128)(2,1)S(1)} %copy-done.1, bf16[2,16,256,128]{3,2,1,0:T(8,128)(2,1)S(1)} %copy-done, s32[256,128]{1,0:T(8,128)S(1)} %copy-done.2), custom_call_target="tpu_custom_call" | custom-call | tf_op jit(solution)/shard_map/pallas_call | solution.py:305
  178.9 3.2 %shard_map.51 = (bf16[2,16,256,128]{3,2,1,0:T(8,128)(2,1)}, bf16[2,16,256,128]{3,2,1,0:T(8,128)(2,1)}) custom-call(bf16[16,256,256]{2,1,0:T(8,128)(2,1)S(1)} %get-tuple-element.4.o_ref, f32[16,8,128]{2,1,0:T(8,128)S(1)} %get-tuple-element.5.filt_ref, bf16[2,16,256,128]{3,2,1,0:T(8,128)(2,1)S(1)} %copy-done, s32[256,128]{1,0:T(8,128)S(1)} %copy-done.2), custom_call_target="tpu_custom_call" | custom-call | tf_op jit(solution)/shard_map/pallas_call | solution.py:340
Async XLA Ops:
  0.6 1.6 copy-start
  2.2 1.6 copy-start.1
  3.8 0.9 copy-start.2

commit v3 on v1

v3 whole, which is shorter than its diff:
```python
import functools

import jax
import jax.numpy as jnp
from jax import lax
from jax.experimental import pallas as pl
from jax.experimental.pallas import tpu as pltpu
from jax.sharding import PartitionSpec as P

MESH = pl.DeviceIdType.MESH


def each(start, stop, body):
    def step(index, carry):
        body(index)
        return carry

    lax.fori_loop(start, stop, step, 0)


def exchange_kernel(
    n_shot, n_rcv,
    d_ref, s_ref, live_ref, o_ref, filt_ref,
    dbuf, pbuf, srec, live_v, rec, mbuf, fbuf, acc,
    load_sem, d_send, d_recv, p_send, p_recv, o_send, o_recv, f_send, f_recv,
):
    n_freq, own_rows = d_ref.shape[1], d_ref.shape[2]
    own_pts, own_shots = s_ref.shape[2], s_ref.shape[3]
    points = own_pts * n_rcv
    per_group = n_freq // n_rcv
    n_groups = n_shot // per_group
    n_dev = n_shot * n_rcv
    me_i, me_j = lax.axis_index("shot"), lax.axis_index("rcv")
    group, place = lax.div(me_i, per_group), lax.rem(me_i, per_group)
    me = me_i * n_rcv + me_j
    my_f = place * n_rcv + me_j

    load_s = pltpu.make_async_copy(s_ref, srec, load_sem.at[0])
    load_live = pltpu.make_async_copy(live_ref, live_v, load_sem.at[1])
    load_s.start()
    load_live.start()

    barrier = pltpu.get_barrier_semaphore()

    def greet(k):
        other = lax.rem(me + k, n_dev)
        pl.semaphore_signal(
            barrier, inc=1, device_id=(lax.div(other, n_rcv), lax.rem(other, n_rcv)), device_id_type=MESH
        )

    each(1, n_dev, greet)
    pl.semaphore_wait(barrier, n_dev - 1)

    def rows_of(i, size):
        return pl.ds(pl.multiple_of(i * size, size), size)

    def send(src, dst, target, send_sem, recv_sem):
        here = jnp.logical_and(target[0] == me_i, target[1] == me_j)

        @pl.when(here)
        def _():
            pltpu.make_async_copy(src, dst, recv_sem).start()

        @pl.when(jnp.logical_not(here))
        def _():
            pltpu.make_async_remote_copy(
                src_ref=src, dst_ref=dst, send_sem=send_sem, recv_sem=recv_sem,
                device_id=target, device_id_type=MESH,
            ).start()

    def sent(src, target, send_sem):
        here = jnp.logical_and(target[0] == me_i, target[1] == me_j)

        @pl.when(jnp.logical_not(here))
        def _():
            pltpu.make_async_copy(src, src, send_sem).wait()

    def arrived(dst, recv_sem):
        pltpu.make_async_copy(dst, dst, recv_sem).wait()

    def target_of(k):
        p = lax.rem(place + lax.div(k, n_rcv), per_group)
        j = lax.rem(me_j + lax.rem(k, n_rcv), n_rcv)
        return p, j, p * n_rcv + j

    def d_block(i, j):
        return dbuf.at[j, :, rows_of(i, own_rows), :]

    def d_target(k, gg):
        p, j, f = target_of(k)
        return (lax.rem(group + gg, n_groups) * per_group + p, j), f

    def send_d(k, gg):
        target, f = d_target(k, gg)
        send(d_ref.at[:, f], d_block(me_i, me_j), target, d_send.at[gg, k], d_recv.at[me_i, me_j])

    def sent_d(n):
        gg, k = lax.div(n, n_freq), lax.rem(n, n_freq)
        target, f = d_target(k, gg)
        sent(d_ref.at[:, f], target, d_send.at[gg, k])

    def send_d_others(k):
        each(1, n_groups, lambda gg: send_d(k, gg))

    def send_p(k):
        p, j, f = target_of(k)
        keep = live_v[...].astype(jnp.bfloat16)
        rec[f, :, :own_shots] = srec[0, f] * keep
        rec[f, :, own_shots:] = srec[1, f] * keep
        dst = pbuf.at[place, rows_of(me_j, own_pts), :]
        send(rec.at[f], dst, (group * per_group + p, j), p_send.at[k], p_recv.at[place, me_j])

    def sent_p(k):
        p, j, f = target_of(k)
        sent(rec.at[f], (group * per_group + p, j), p_send.at[k])

    early, middle = 2, n_freq // 2
    each(0, early, send_d_others)
    load_s.wait()
    load_live.wait()

    def send_first(k):
        send_p(2 * k)
        send_p(2 * k + 1)
        send_d_others(k + early)

    def send_own(k):
        send_d(2 * (k - middle), 0)
        send_d(2 * (k - middle) + 1, 0)

    def send_second(k):
        send_own(k)
        send_d_others(k + early)

    each(0, middle, send_first)
    each(middle, n_freq - early, send_second)
    each(n_freq - early, n_freq, send_own)

    def records_arrived(n):
        b, j = lax.div(n, n_rcv), lax.rem(n, n_rcv)
        arrived(pbuf.at[b, rows_of(j, own_pts), :], p_recv.at[b, j])

    acc[...] = jnp.zeros_like(acc)
    each(0, n_freq, records_arrived)

    def o_src(b, i):
        return mbuf.at[b, rows_of(i, own_rows), :]

    per_rcv = own_pts // own_rows

    def compute(i):
        rows = rows_of(i, own_rows)
        j = lax.div(i, per_rcv)

        def arrival(h):
            arrived(d_block(i, h), d_recv.at[i, h])

        each(0, n_rcv, arrival)

        def one(n):
            b = lax.rem(n + place, per_group)
            total = None
            for h in range(n_rcv):
                block = pbuf[b, h * own_pts:(h + 1) * own_pts, :]
                left = dbuf[h, :, rows, :].reshape(2 * own_rows, own_pts)
                prod = jnp.dot(left, block, preferred_element_type=jnp.float32)
                total = prod if total is None else total + prod
            m_re = total[:own_rows, :own_shots] - total[own_rows:, own_shots:]
            m_im = total[:own_rows, own_shots:] + total[own_rows:, :own_shots]
            mbuf[b, rows, :own_shots] = m_re.astype(jnp.bfloat16)
            mbuf[b, rows, own_shots:] = m_im.astype(jnp.bfloat16)
            dst = o_ref.at[my_f, rows_of(lax.rem(i, per_rcv), own_rows), :]
            send(o_src(b, i), dst, (group * per_group + b, j), o_send.at[b, j], o_recv.at[my_f])
            p_re = pbuf[b, rows, :own_shots].astype(jnp.float32)
            p_im = pbuf[b, rows, own_shots:].astype(jnp.float32)

            def down(value):
                return jnp.sum(value.reshape(own_rows // 8, 8, own_shots), axis=0)

            acc[b, 0] += down(m_re * p_re + m_im * p_im)
            acc[b, 1] += down(m_re * p_im - m_im * p_re)
            acc[b, 2] += down(m_re * m_re + m_im * m_im)

        each(0, per_group, one)

    turns = [((t + 1) * n_rcv, 0, t) for t in range(per_group)]
    turns += [(middle + (t + 1) * n_rcv // 2, 1, t) for t in range(per_group)]
    for _, own, t in sorted(turns):
        p = lax.rem(place + per_group - t, per_group)
        if own:
            compute(group * per_group + p)
        else:
            each(1, n_groups, lambda gg: compute(lax.rem(group + gg, n_groups) * per_group + p))

    def coefficients(n):
        b = lax.rem(n + place, per_group)
        num_re, num_im, power = (
            jnp.sum(acc[b, v], axis=0, keepdims=True) / float(points) for v in range(3)
        )
        power = power + 1e-6
        row = lax.broadcasted_iota(jnp.int32, (8, own_shots), 0)
        fbuf[b] = jnp.where(row < 4, num_re / power, num_im / power)
        for j in range(n_rcv):
            send(fbuf.at[b], filt_ref.at[my_f], (group * per_group + b, j), f_send.at[b, j], f_recv.at[my_f])

    each(0, per_group, coefficients)

    def sent_results(n):
        b, j = lax.div(n, n_rcv), lax.rem(n, n_rcv)
        target = (group * per_group + b, j)
        sent(fbuf.at[b], target, f_send.at[b, j])
        sent(mbuf.at[b, rows_of(j, own_pts), :], target, o_send.at[b, j])

    def result_arrived(n):
        arrived(o_ref.at[n], o_recv.at[n])
        arrived(filt_ref.at[n], f_recv.at[n])

    each(0, n_freq, result_arrived)
    each(0, n_freq * n_groups, sent_d)
    each(0, n_freq, sent_p)
    each(0, per_group * n_rcv, sent_results)


def subtract_kernel(o_ref, filt_ref, s_ref, live_ref, pred_ref, prim_ref):
    shots = s_ref.shape[3]
    keep = live_ref[...].astype(jnp.bfloat16)
    for f in range(o_ref.shape[0]):
        re, im = o_ref[f, :, :shots], o_ref[f, :, shots:]
        pred_ref[0, f] = re
        pred_ref[1, f] = im
        re, im = re.astype(jnp.float32), im.astype(jnp.float32)
        filt_re, filt_im = filt_ref[f, 0:1, :], filt_ref[f, 4:5, :]
        rec_re = (s_ref[0, f] * keep).astype(jnp.float32)
        rec_im = (s_ref[1, f] * keep).astype(jnp.float32)
        prim_ref[0, f] = (rec_re - (filt_re * re - filt_im * im)).astype(jnp.bfloat16)
        prim_ref[1, f] = (rec_im - (filt_re * im + filt_im * re)).astype(jnp.bfloat16)


def shards(n_shot, n_rcv, data_matrix, shot_records, live):
    _, n_freq, own_rows, own_pts = data_matrix.shape
    own_shots = shot_records.shape[3]
    points = own_pts * n_rcv
    per_group = n_freq // n_rcv
    n_groups = n_shot // per_group
    anywhere = pl.BlockSpec(memory_space=pl.ANY)
    dma = pltpu.SemaphoreType.DMA
    multiples, filt = pl.pallas_call(
        functools.partial(exchange_kernel, n_shot, n_rcv),
        out_shape=(
            jax.ShapeDtypeStruct((n_freq, own_pts, 2 * own_shots), jnp.bfloat16),
            jax.ShapeDtypeStruct((n_freq, 8, own_shots), jnp.float32),
        ),
        in_specs=[anywhere] * 3,
        out_specs=(anywhere, anywhere),
        scratch_shapes=[
            pltpu.VMEM((n_rcv, 2, points, own_pts), jnp.bfloat16),
            pltpu.VMEM((per_group, points, 2 * own_shots), jnp.bfloat16),
            pltpu.VMEM((2, n_freq, own_pts, own_shots), jnp.bfloat16),
            pltpu.VMEM((own_pts, own_shots), jnp.int32),
            pltpu.VMEM((n_freq, own_pts, 2 * own_shots), jnp.bfloat16),
            pltpu.VMEM((per_group, points, 2 * own_shots), jnp.bfloat16),
            pltpu.VMEM((per_group, 8, own_shots), jnp.float32),
            pltpu.VMEM((per_group, 3, 8, own_shots), jnp.float32),
            dma((2,)),
            dma((n_groups, n_freq)),
            dma((n_shot, n_rcv)),
            dma((n_freq,)),
            dma((per_group, n_rcv)),
            dma((per_group, n_rcv)),
            dma((n_freq,)),
            dma((per_group, n_rcv)),
            dma((n_freq,)),
        ],
        compiler_params=pltpu.CompilerParams(
            collective_id=0, has_side_effects=True, vmem_limit_bytes=60 * 1024 * 1024
        ),
    )(data_matrix, shot_records, live)
    step = 4
    pair = pl.BlockSpec((2, step, own_pts, own_shots), lambda f: (0, f, 0, 0))
    out = jax.ShapeDtypeStruct((2, n_freq, own_pts, own_shots), jnp.bfloat16)
    return pl.pallas_call(
        subtract_kernel,
        grid=(n_freq // step,),
        out_shape=(out, out),
        in_specs=[
            pl.BlockSpec((step, own_pts, 2 * own_shots), lambda f: (f, 0, 0)),
            pl.BlockSpec((step, 8, own_shots), lambda f: (f, 0, 0)),
            pair,
            pl.BlockSpec((own_pts, own_shots), lambda f: (0, 0)),
        ],
        out_specs=(pair, pair),
        compiler_params=pltpu.CompilerParams(vmem_limit_bytes=24 * 1024 * 1024),
    )(multiples, filt, shot_records, live)


def solution(mesh):
    in_specs = (P(None, None, "shot", "rcv"), P(None, None, "rcv", "shot"), P("rcv", "shot"))
    out_specs = (P(None, None, "rcv", "shot"), P(None, None, "rcv", "shot"))
    body = functools.partial(shards, mesh.shape["shot"], mesh.shape["rcv"])
    return jax.shard_map(body, mesh=mesh, in_specs=in_specs, out_specs=out_specs, check_vma=False)
```

time: 156 us -> 141 us (0.904)
  the two profiles are of different devices: /device:TPU:5 before, /device:TPU:15 now
where the time goes in v3:
time: 141 us; the launch traced here: 140 us
  Pallas kernels  137 us (97%)
  local copies, waits for them, and re-layouts  2.43 us (2%)
    pallas_call x1, Pallas kernels, shards(): pl.pallas_call(functools.partial(exchange_kernel, n_shot, n_rcv), out_sha...  134 us
    pallas_call x1, Pallas kernels, shards(): pl.pallas_call(subtract_kernel, grid=(n_freq // step,), out_shape=(out, o...  3.19 us

profile of v3, /device:TPU:15, one launch (start us, length us, event | category | flops | bytes accessed | tf_op | source)
XLA Modules:
  0.0 140.5 jit_solution(12982482087430992990)
XLA Ops:
  0.6 0.0 copy-start.2
  0.6 0.0 copy-start
  0.6 134.2 %shard_map.50 = (bf16[16,256,256]{2,1,0:T(8,128)(2,1)}, f32[16,8,128]{2,1,0:T(8,128)}) custom-call(bf16[2,16,128,256]{3,2,1,0:T(8,128)(2,1)} %d_ref.1, bf16[2,16,256,128]{3,2,1,0:T(8,128)(2,1)} %s_ref.3, s32[256,128]{1,0:T(8,128)} %live_ref.3), custom_call_target="tpu_custom_call" | custom-call | tf_op jit(solution)/shard_map/pallas_call | solution.py:247
  134.8 0.0 copy-done.2
  134.8 0.0 copy-done
  134.8 0.0 copy-start.1
  134.8 1.6 %copy-done.1 = bf16[16,256,256]{2,1,0:T(8,128)(2,1)S(1)} copy-done((bf16[16,256,256]{2,1,0:T(8,128)(2,1)S(1)}, bf16[16,256,256]{2,1,0:T(8,128)(2,1)}, u32[]{:S(2)}) %copy-start.1) | copy-done | bytes 2097176
  136.4 0.0 copy-start.3
  136.4 0.8 copy-done.3
  137.3 3.2 %shard_map.51 = (bf16[2,16,256,128]{3,2,1,0:T(8,128)(2,1)}, bf16[2,16,256,128]{3,2,1,0:T(8,128)(2,1)}) custom-call(bf16[16,256,256]{2,1,0:T(8,128)(2,1)S(1)} %copy-done.1, f32[16,8,128]{2,1,0:T(8,128)S(1)} %copy-done.3, bf16[2,16,256,128]{3,2,1,0:T(8,128)(2,1)S(1)} %copy-done, s32[256,128]{1,0:T(8,128)S(1)} %copy-done.2), custom_call_target="tpu_custom_call" | custom-call | tf_op jit(solution)/shard_map/pallas_call | solution.py:281
Async XLA Ops:
  0.6 134.2 %copy-start.2 = (s32[256,128]{1,0:T(8,128)S(1)}, s32[256,128]{1,0:T(8,128)}, u32[]{:S(2)}) copy-start(s32[256,128]{1,0:T(8,128)} %live_ref.3) | copy-start | bytes 393220
  0.6 134.2 %copy-start = (bf16[2,16,256,128]{3,2,1,0:T(8,128)(2,1)S(1)}, bf16[2,16,256,128]{3,2,1,0:T(8,128)(2,1)}, u32[]{:S(2)}) copy-start(bf16[2,16,256,128]{3,2,1,0:T(8,128)(2,1)} %s_ref.3) | copy-start | bytes 6291460
  134.8 1.6 %copy-start.1 = (bf16[16,256,256]{2,1,0:T(8,128)(2,1)S(1)}, bf16[16,256,256]{2,1,0:T(8,128)(2,1)}, u32[]{:S(2)}) copy-start(bf16[16,256,256]{2,1,0:T(8,128)(2,1)} %get-tuple-element.4.o_ref) | copy-start | bytes 6291460
  136.4 0.8 copy-start.3

commit v4 on v3

--- a/solution.py
+++ b/solution.py
@@ -119,22 +119,19 @@
     load_s.wait()
     load_live.wait()
 
-    def send_first(k):
+    def send_records(k):
         send_p(2 * k)
         send_p(2 * k + 1)
         send_d_others(k + early)
-
-    def send_own(k):
-        send_d(2 * (k - middle), 0)
-        send_d(2 * (k - middle) + 1, 0)
-
-    def send_second(k):
-        send_own(k)
+        send_d(k, 0)
+
+    def send_rest(k):
         send_d_others(k + early)
-
-    each(0, middle, send_first)
-    each(middle, n_freq - early, send_second)
-    each(n_freq - early, n_freq, send_own)
+        send_d(k, 0)
+
+    each(0, middle, send_records)
+    each(middle, n_freq - early, send_rest)
+    each(n_freq - early, n_freq, lambda k: send_d(k, 0))
 
     def records_arrived(n):
         b, j = lax.div(n, n_rcv), lax.rem(n, n_rcv)
@@ -184,7 +181,7 @@
         each(0, per_group, one)
 
     turns = [((t + 1) * n_rcv, 0, t) for t in range(per_group)]
-    turns += [(middle + (t + 1) * n_rcv // 2, 1, t) for t in range(per_group)]
+    turns += [((t + 1) * n_rcv, 1, t) for t in range(per_group)]
     for _, own, t in sorted(turns):
         p = lax.rem(place + per_group - t, per_group)
         if own:

time: 141 us -> 138 us (0.979)
  Pallas kernels: 137 us -> 134 us
    pallas_call x1, Pallas kernels: 134 us -> 131 us  [shards(): pl.pallas_call(functools.partial(exchange_kernel, n_shot, n_rcv), out_sha...]
where the time goes in v4:
time: 138 us
  Pallas kernels  134 us (97%)
  local copies, waits for them, and re-layouts  2.43 us (2%)
    pallas_call x1, Pallas kernels, shards(): pl.pallas_call(functools.partial(exchange_kernel, n_shot, n_rcv), out_sha...  131 us
    pallas_call x1, Pallas kernels, shards(): pl.pallas_call(subtract_kernel, grid=(n_freq // step,), out_shape=(out, o...  3.19 us

profile of v4, /device:TPU:15, one launch (start us, length us, event | category | flops | bytes accessed | tf_op | source)
XLA Modules:
  0.0 137.6 jit_solution(5854022571142864177)
XLA Ops:
  0.6 0.0 copy-start.2
  0.6 0.0 copy-start
  0.6 131.3 %shard_map.50 = (bf16[16,256,256]{2,1,0:T(8,128)(2,1)}, f32[16,8,128]{2,1,0:T(8,128)}) custom-call(bf16[2,16,128,256]{3,2,1,0:T(8,128)(2,1)} %d_ref.1, bf16[2,16,256,128]{3,2,1,0:T(8,128)(2,1)} %s_ref.3, s32[256,128]{1,0:T(8,128)} %live_ref.3), custom_call_target="tpu_custom_call" | custom-call | tf_op jit(solution)/shard_map/pallas_call | solution.py:244
  131.9 0.0 copy-done.2
  132.0 0.0 copy-done
  132.0 0.0 copy-start.1
  132.0 1.6 %copy-done.1 = bf16[16,256,256]{2,1,0:T(8,128)(2,1)S(1)} copy-done((bf16[16,256,256]{2,1,0:T(8,128)(2,1)S(1)}, bf16[16,256,256]{2,1,0:T(8,128)(2,1)}, u32[]{:S(2)}) %copy-start.1) | copy-done | bytes 2097176
  133.6 0.0 copy-start.3
  133.6 0.8 copy-done.3
  134.4 3.2 %shard_map.51 = (bf16[2,16,256,128]{3,2,1,0:T(8,128)(2,1)}, bf16[2,16,256,128]{3,2,1,0:T(8,128)(2,1)}) custom-call(bf16[16,256,256]{2,1,0:T(8,128)(2,1)S(1)} %copy-done.1, f32[16,8,128]{2,1,0:T(8,128)S(1)} %copy-done.3, bf16[2,16,256,128]{3,2,1,0:T(8,128)(2,1)S(1)} %copy-done, s32[256,128]{1,0:T(8,128)S(1)} %copy-done.2), custom_call_target="tpu_custom_call" | custom-call | tf_op jit(solution)/shard_map/pallas_call | solution.py:278
Async XLA Ops:
  0.6 131.3 %copy-start.2 = (s32[256,128]{1,0:T(8,128)S(1)}, s32[256,128]{1,0:T(8,128)}, u32[]{:S(2)}) copy-start(s32[256,128]{1,0:T(8,128)} %live_ref.3) | copy-start | bytes 393220
  0.6 131.3 %copy-start = (bf16[2,16,256,128]{3,2,1,0:T(8,128)(2,1)S(1)}, bf16[2,16,256,128]{3,2,1,0:T(8,128)(2,1)}, u32[]{:S(2)}) copy-start(bf16[2,16,256,128]{3,2,1,0:T(8,128)(2,1)} %s_ref.3) | copy-start | bytes 6291460
  132.0 1.6 %copy-start.1 = (bf16[16,256,256]{2,1,0:T(8,128)(2,1)S(1)}, bf16[16,256,256]{2,1,0:T(8,128)(2,1)}, u32[]{:S(2)}) copy-start(bf16[16,256,256]{2,1,0:T(8,128)(2,1)} %get-tuple-element.4.o_ref) | copy-start | bytes 6291460
  133.6 0.8 copy-start.3

commit v5 on v4

--- a/solution.py
+++ b/solution.py
@@ -114,14 +114,14 @@
         p, j, f = target_of(k)
         sent(rec.at[f], (group * per_group + p, j), p_send.at[k])
 
-    early, middle = 2, n_freq // 2
+    early = 2
     each(0, early, send_d_others)
     load_s.wait()
     load_live.wait()
 
     def send_records(k):
-        send_p(2 * k)
-        send_p(2 * k + 1)
+        for n in range(4):
+            send_p(4 * k + n)
         send_d_others(k + early)
         send_d(k, 0)
 
@@ -129,8 +129,8 @@
         send_d_others(k + early)
         send_d(k, 0)
 
-    each(0, middle, send_records)
-    each(middle, n_freq - early, send_rest)
+    each(0, n_freq // 4, send_records)
+    each(n_freq // 4, n_freq - early, send_rest)
     each(n_freq - early, n_freq, lambda k: send_d(k, 0))
 
     def records_arrived(n):

time: 138 us -> 138 us (level)
  no operation moved by 1% of the time
where the time goes in v5:
time: 138 us; the launch traced here: 137 us
  Pallas kernels  134 us (97%)
  local copies, waits for them, and re-layouts  2.43 us (2%)
    pallas_call x1, Pallas kernels, shards(): pl.pallas_call(functools.partial(exchange_kernel, n_shot, n_rcv), out_sha...  130 us
    pallas_call x1, Pallas kernels, shards(): pl.pallas_call(subtract_kernel, grid=(n_freq // step,), out_shape=(out, o...  3.19 us

profile of v5, /device:TPU:15, one launch (start us, length us, event | category | flops | bytes accessed | tf_op | source)
XLA Modules:
  0.0 136.8 jit_solution(609478756251806502)
XLA Ops:
  0.6 0.0 copy-start.2
  0.6 0.0 copy-start
  0.6 130.5 %shard_map.50 = (bf16[16,256,256]{2,1,0:T(8,128)(2,1)}, f32[16,8,128]{2,1,0:T(8,128)}) custom-call(bf16[2,16,128,256]{3,2,1,0:T(8,128)(2,1)} %d_ref.1, bf16[2,16,256,128]{3,2,1,0:T(8,128)(2,1)} %s_ref.3, s32[256,128]{1,0:T(8,128)} %live_ref.3), custom_call_target="tpu_custom_call" | custom-call | tf_op jit(solution)/shard_map/pallas_call | solution.py:244
  131.2 0.0 copy-done.2
  131.2 0.0 copy-done
  131.2 0.0 copy-start.1
  131.2 1.6 %copy-done.1 = bf16[16,256,256]{2,1,0:T(8,128)(2,1)S(1)} copy-done((bf16[16,256,256]{2,1,0:T(8,128)(2,1)S(1)}, bf16[16,256,256]{2,1,0:T(8,128)(2,1)}, u32[]{:S(2)}) %copy-start.1) | copy-done | bytes 2097176
  132.8 0.0 copy-start.3
  132.8 0.8 copy-done.3
  133.6 3.2 %shard_map.51 = (bf16[2,16,256,128]{3,2,1,0:T(8,128)(2,1)}, bf16[2,16,256,128]{3,2,1,0:T(8,128)(2,1)}) custom-call(bf16[16,256,256]{2,1,0:T(8,128)(2,1)S(1)} %copy-done.1, f32[16,8,128]{2,1,0:T(8,128)S(1)} %copy-done.3, bf16[2,16,256,128]{3,2,1,0:T(8,128)(2,1)S(1)} %copy-done, s32[256,128]{1,0:T(8,128)S(1)} %copy-done.2), custom_call_target="tpu_custom_call" | custom-call | tf_op jit(solution)/shard_map/pallas_call | solution.py:278
Async XLA Ops:
  0.6 130.5 %copy-start.2 = (s32[256,128]{1,0:T(8,128)S(1)}, s32[256,128]{1,0:T(8,128)}, u32[]{:S(2)}) copy-start(s32[256,128]{1,0:T(8,128)} %live_ref.3) | copy-start | bytes 393220
  0.6 130.5 %copy-start = (bf16[2,16,256,128]{3,2,1,0:T(8,128)(2,1)S(1)}, bf16[2,16,256,128]{3,2,1,0:T(8,128)(2,1)}, u32[]{:S(2)}) copy-start(bf16[2,16,256,128]{3,2,1,0:T(8,128)(2,1)} %s_ref.3) | copy-start | bytes 6291460
  131.2 1.6 %copy-start.1 = (bf16[16,256,256]{2,1,0:T(8,128)(2,1)S(1)}, bf16[16,256,256]{2,1,0:T(8,128)(2,1)}, u32[]{:S(2)}) copy-start(bf16[16,256,256]{2,1,0:T(8,128)(2,1)} %get-tuple-element.4.o_ref) | copy-start | bytes 6291460
  132.8 0.8 copy-start.3
